TPU v7x, 32 devices: a whole 2x2x4 slice. The times are simulated.
32 devices in a mesh: groups: 2 (over y), seq: 4 (over z), mp: 2 (over x), section: 2 (over core).
Axes of the slice: x: 2, y: 2, z: 4, core: 2. Of those that a mesh axis runs over, the one named last changes fastest.
Arguments:
- features: bfloat16 [4, 512, 8192], P(('groups', 'section'), 'mp', 'seq'), parts along dimension 0, may hold values from -6 to 6
- alpha: float32 [512], P('mp'), may hold values from 0.5 to 2
- conv_weight: bfloat16 [1024, 32, 16], P('mp'), may hold values from -0.25 to 0.25
- qkv_weight: bfloat16 [1024, 3, 1024], P(None, None, 'mp'), may hold values from -1 to 1
- readout: float32 [1024], P('mp'), may hold values from -4 to 4
- offsets: int32 [4], P(('groups', 'section')), parts along dimension 0, may hold values from 0 to 14479
- pairs: int32 [8, 2], P('groups'), parts along dimension 0, may hold values from 0 to 1
- labels: int32 [8], P('groups'), parts along dimension 0, may hold values from 0 to 1
Outputs:
- grads: bfloat16 [3, 4, 1024, 1024], P(None, ('groups', 'section'), 'seq', 'mp'), parts along dimension 1
- rewards: float32 [4], P('groups'), parts along dimension 0
- loss: float32 [2], P('groups'), parts along dimension 0
There are 2 independent parts, one for each index of `groups`. A program takes and returns all parts, laid end to end along the dimension named above; an argument that names none is the same for every part. Nothing has to cross between parts.
All inputs are finite; a program needn't handle non-finite values.
Results may differ from a plain program's by a relative error of at most 0.017.
Values may be sent and summed in bfloat16 or wider, within the bound.
A program may use at most 64 MiB of HBM per device.

v0:
```python
import math
import jax
import jax.numpy as jnp
from jax import lax
from jax.sharding import PartitionSpec as P

D = 1024
HD = 64
EPS = 1e-06
BASE = 10000.0


def padded_2(block, sides, width):
    for axis, dim in sides:
        count = lax.axis_size(axis)
        forward = [(i, i + 1) for i in range(count - 1)]
        backward = [(target, source) for source, target in forward]
        low = lax.ppermute(
            lax.slice_in_dim(block, block.shape[dim] - width, None, axis=dim), axis, forward
        )
        high = lax.ppermute(lax.slice_in_dim(block, 0, width, axis=dim), axis, backward)
        block = jnp.concatenate([low, block, high], axis=dim)
    return block


def position_table(positions, feature_ids, width):
    pair_ids = (feature_ids // 2).astype(jnp.float32)
    freqs = jnp.exp(pair_ids * (-2.0 * math.log(BASE) / width))
    angle = positions.astype(jnp.float32)[..., None] * freqs
    return jnp.where(feature_ids % 2 == 0, jnp.sin(angle), jnp.cos(angle))


def local(features, alpha, conv_weight, qkv_weight, readout, offsets, pairs, labels):
    f32 = jnp.float32
    bf16 = jnp.bfloat16
    cand, chans, samples = features.shape
    local_width = conv_weight.shape[0]
    per_group = conv_weight.shape[1]
    kern = conv_weight.shape[2]
    stride = kern // 2
    frames_dev = samples // stride
    groups_here = chans // per_group
    heads_here = local_width // HD
    raw = features.astype(f32)
    slope = alpha[None, :, None]
    act = (raw + jnp.sin(slope * raw) ** 2 / slope).astype(bf16)
    padded = padded_2(act, (("seq", 2),), stride // 2)
    blocks = padded.reshape(cand, groups_here, per_group, frames_dev + 1, stride).transpose(
        0, 1, 3, 2, 4
    )
    patches = jnp.concatenate([blocks[:, :, :-1], blocks[:, :, 1:]], axis=-1).reshape(
        cand, groups_here, frames_dev, per_group * kern
    )
    kernel = conv_weight.reshape(groups_here, local_width // groups_here, per_group * kern)
    frames = jnp.einsum("cgfk,gok->cfgo", patches, kernel, preferred_element_type=f32).reshape(
        cand, frames_dev, local_width
    )
    slice_id = lax.axis_index("seq")
    part_id = lax.axis_index("mp")
    positions = (
        offsets[:, None] + slice_id * frames_dev + jnp.arange(frames_dev, dtype=jnp.int32)[None, :]
    )
    feature_ids = part_id * local_width + jnp.arange(local_width, dtype=jnp.int32)
    resid = (frames + position_table(positions, feature_ids, D)).astype(bf16)
    whole = lax.all_gather(resid, "mp", axis=2, tiled=True)
    squares = jnp.mean(jnp.square(whole.astype(f32)), axis=-1)
    projected = jnp.einsum("cfd,dtk->cftk", whole, qkv_weight, preferred_element_type=f32)
    qkv = (projected * lax.rsqrt(squares + EPS)[:, :, None, None]).astype(bf16)
    query = qkv[:, :, 0]
    keys, values = (
        lax.all_gather(qkv[:, :, 1], "seq", axis=1, tiled=True),
        lax.all_gather(qkv[:, :, 2], "seq", axis=1, tiled=True),
    )
    total = keys.shape[1]
    block = min(512, total)
    count_blocks = total // block
    scale = 1.0 / math.sqrt(HD)
    query4 = query.reshape(cand, frames_dev, heads_here, HD)

    def key_slice(source, start, size):
        return lax.dynamic_slice_in_dim(source, start, size, 1).reshape(cand, size, heads_here, HD)

    def scores_for(start, size):
        return (
            jnp.einsum(
                "cfhe,ckhe->chfk", query4, key_slice(keys, start, size), preferred_element_type=f32
            )
            * scale
        )

    def stat_step(carry, index):
        peak_now, mass_now = carry
        score = scores_for(index * block, block)
        fresh = jnp.maximum(peak_now, jnp.max(score, axis=-1))
        mass_now = mass_now * jnp.exp(peak_now - fresh) + jnp.sum(
            jnp.exp(score - fresh[..., None]), axis=-1
        )
        return ((fresh, mass_now), None)

    start_peak = jnp.full((cand, heads_here, frames_dev), -jnp.inf, f32)
    (peak, mass), _ = lax.scan(
        stat_step, (start_peak, jnp.zeros_like(start_peak)), jnp.arange(count_blocks)
    )

    def weights_for(start, size):
        return jnp.exp(scores_for(start, size) - peak[..., None]) / mass[..., None]

    def out_step(running, index):
        start = index * block
        prob = weights_for(start, block).astype(bf16)
        running = running + jnp.einsum(
            "chfk,ckhe->cfhe", prob, key_slice(values, start, block), preferred_element_type=f32
        )
        return (running, None)

    attended4, _ = lax.scan(
        out_step, jnp.zeros((cand, frames_dev, heads_here, HD), f32), jnp.arange(count_blocks)
    )
    attended = attended4.reshape(cand, frames_dev, local_width)
    gate = jax.nn.sigmoid(lax.optimization_barrier(resid).astype(f32))
    section_id = lax.axis_index("section")
    all_cands = cand * lax.axis_size("section")
    owner = (
        jnp.arange(all_cands, dtype=jnp.int32)[None, :]
        == (section_id * cand + jnp.arange(cand, dtype=jnp.int32))[:, None]
    ).astype(f32)
    partial_rewards = jnp.sum(attended * gate * readout, axis=(1, 2)) / math.sqrt(total)
    rewards = lax.psum(jnp.sum(owner * partial_rewards[:, None], axis=0), ("seq", "mp", "section"))
    chosen = (pairs[:, :, None] == jnp.arange(all_cands, dtype=jnp.int32)[None, None, :]).astype(
        f32
    )
    paired = jnp.sum(chosen * rewards[None, None, :], axis=-1)
    margin = paired[:, 0] - paired[:, 1]
    target = labels.astype(f32)
    loss = jnp.sum(jax.nn.softplus(margin) - target * margin)
    coeff = jax.nn.sigmoid(margin) - target
    reward_grad = jnp.sum(coeff[:, None] * (chosen[:, 0] - chosen[:, 1]), axis=0)
    own_grad = jnp.sum(owner * reward_grad[None, :], axis=1)
    upstream = (own_grad[:, None, None] * readout * gate).astype(bf16)
    upstream4 = upstream.reshape(cand, frames_dev, heads_here, HD)
    delta = jnp.sum(upstream4.astype(f32) * attended4, axis=-1).transpose(0, 2, 1)

    def backward_block(start, size):
        prob = weights_for(start, size)
        prob_low = prob.astype(bf16)
        dprob = jnp.einsum(
            "cfhe,ckhe->chfk", upstream4, key_slice(values, start, size), preferred_element_type=f32
        )
        dscore = (prob * (dprob - delta[..., None])).astype(bf16)
        dquery = (
            jnp.einsum(
                "chfk,ckhe->cfhe", dscore, key_slice(keys, start, size), preferred_element_type=f32
            )
            * scale
        )
        dkey = jnp.einsum("chfk,cfhe->kche", dscore, query4, preferred_element_type=f32) * scale
        dvalue = jnp.einsum("chfk,cfhe->kche", prob_low, upstream4, preferred_element_type=f32)
        term = jnp.concatenate(
            [dkey.reshape(size, cand, local_width), dvalue.reshape(size, cand, local_width)],
            axis=-1,
        )
        return (dquery, term)

    zero_query = jnp.zeros((cand, frames_dev, heads_here, HD), f32)

    def grad_step(running, index):
        dquery, term = backward_block(index * block, block)
        return (running + dquery, term.astype(bf16))

    grad_query, stored = lax.scan(grad_step, zero_query, jnp.arange(count_blocks))
    stacked = stored.reshape(total, cand, 2 * local_width)
    summed = lax.psum_scatter(
        stacked.astype(f32).astype(jnp.bfloat16), "seq", scatter_dimension=0, tiled=True
    ).astype(jnp.float32)
    grad_key = summed[:, :, :local_width].transpose(1, 0, 2)
    grad_value = summed[:, :, local_width:].transpose(1, 0, 2)
    grads = jnp.stack(
        [grad_query.reshape(cand, frames_dev, local_width), grad_key, grad_value], axis=0
    ).astype(bf16)
    return (grads, rewards, loss.reshape(1))


def solution(mesh):
    placed = (
        P(("groups", "section"), "mp", "seq"),
        P("mp"),
        P("mp", None, None),
        P(None, None, "mp"),
        P("mp"),
        P(("groups", "section")),
        P("groups", None),
        P("groups"),
    )
    return jax.shard_map(
        local,
        mesh=mesh,
        in_specs=placed,
        out_specs=(P(None, ("groups", "section"), "seq", "mp"), P("groups"), P("groups")),
        check_vma=False,
    )
```

profile of v0, /device:TPU:0, one launch (start us, length us, event | category | flops | bytes accessed | tf_op | source)
XLA Modules:
  0.0 278.7 jit_solution(6267920341593110061)
XLA Ops:
  7.2 8.6 %fusion.25 = bf16[1,256,2048]{2,1,0:T(8,128)(2,1)S(1)} fusion(bf16[1,256,2048]{2,1,0:T(8,128)(2,1)} %param.14, f32[256]{0:T(256)} %param.15), kind=kLoop, calls=%fused_computation.40 | loop fusion | flops 3145728 | bytes 2098176 | tf_op jit(solution)/shard_map/convert_element_type | solution.py:46
  17.0 4.9 %collective-permute-start = (bf16[1,256,4]{2,1,0:T(8,128)(2,1)S(1)}, bf16[1,256,4]{2,1,0:T(8,128)(2,1)S(1)}, u32[]{:S(2)}, u32[]{:S(2)}) collective-permute-start(bf16[1,256,4]{2,1,0:T(8,128)(2,1)S(1)} %get-tuple-element.365), channel_id=1, source_target_pairs={{0,4},{4,8},{8,12},{1,5},{5,9},{9,13},{2,6},{6,10},{10,14},{3,7},{... | collective-permute-start | bytes 6152 | tf_op jit(solution)/shard_map/ppermute | solution.py:18
  24.1 2.4 reshape.438
  28.1 3.5 %concatenate.32 = bf16[1,256,2056]{2,1,0:T(8,128)(2,1)} concatenate(bf16[1,256,4]{2,1,0:T(8,128)(2,1)S(1)} %collective-permute-done, bf16[1,256,2048]{2,1,0:T(8,128)(2,1)} %copy-done.5, bf16[1,256,4]{2,1,0:T(8,128)(2,1)S(1)} %collective-permute-done.1), dimensions={2} | concatenate | bytes 2105344 | tf_op jit(solution)/shard_map/concatenate | solution.py:22
  31.6 2.3 copy.41
  33.9 5.8 %reshape.436 = bf16[1,8,32,257,8]{2,1,4,3,0:T(8,128)(2,1)} reshape(bf16[1,256,2056]{1,2,0:T(8,128)(2,1)} %copy.41) | data formatting | bytes 2105344 | tf_op jit(solution)/shard_map/reshape | solution.py:48
  39.7 6.5 %fusion.53 = (bf16[1,8,256,32,8]{3,1,4,2,0:T(8,128)(2,1)}, bf16[1,8,256,32,8]{3,1,4,2,0:T(8,128)(2,1)}) fusion(bf16[1,8,257,32,8]{3,1,4,2,0:T(8,128)(2,1)} %bitcast.233), kind=kLoop, calls=%fused_computation.102 | loop fusion | bytes 4194304 | tf_op jit(solution)/shard_map/slice | solution.py:51
  46.2 7.7 %copy.42 = bf16[1,8,256,32,8]{2,4,3,1,0:T(8,128)(2,1)} copy(bf16[1,8,256,32,8]{3,1,4,2,0:T(8,128)(2,1)} %get-tuple-element.362) | data formatting | bytes 2097152 | tf_op jit(solution)/shard_map/slice | solution.py:51
  53.9 7.7 %copy.43 = bf16[1,8,256,32,8]{2,4,3,1,0:T(8,128)(2,1)} copy(bf16[1,8,256,32,8]{3,1,4,2,0:T(8,128)(2,1)} %get-tuple-element.363) | data formatting | bytes 2097152 | tf_op jit(solution)/shard_map/slice | solution.py:51
  66.9 3.5 %fusion.31 = bf16[1,256,512]{2,1,0:T(8,128)(2,1)S(1)} fusion(f32[1,256,512]{2,1,0:T(8,128)} %copy.46, f32[512]{0:T(512)S(1)} %fusion.36, f32[256]{0:T(256)S(1)} %add_convert_fusion, pred[512]{0:T(512)(128)(4,1)S(1)} %fusion.33), kind=kLoop, calls=%fused_computation.52 | loop fusion | flops 524288 | bytes 790016 | tf_op jit(solution)/shard_map/convert_element_type | solution.py:64
  71.1 7.3 %all_gather.9 = bf16[1,256,1024]{2,1,0:T(8,128)(2,1)S(1)} all-gather(bf16[1,256,512]{2,1,0:T(8,128)(2,1)S(1)} %fusion.31), channel_id=1, replica_groups=mesh['groups'=2,'seq'=4,'mp'=2,'section'=2] {'mp'}, dimensions={2}, use_global_device_ids=true | all-gather | bytes 786432 | tf_op jit(solution)/shard_map/all_gather | solution.py:65
  82.1 28.3 %all-gather.5.cloned.1.call-done = bf16[1,1024,1,512]{3,1,2,0:T(8,128)(2,1)} async-done(((bf16[1,256,1,512]{3,1,2,0:T(8,128)(2,1)}), bf16[1,1024,1,512]{3,1,2,0:T(8,128)(2,1)}) %all-gather.5.cloned.1.call-update) | async-done | bytes 1048592 | tf_op jit(solution)/shard_map/all_gather | solution.py:71
  110.4 2.3 copy.53
  112.6 16.1 %while.37 = (s32[]{:T(128)}, f32[1,8,256]{2,1,0:T(8,128)S(1)}, f32[1,8,256]{2,1,0:T(8,128)S(1)}, s32[2]{0:T(128)S(1)}, bf16[1,1024,512]{1,2,0:T(8,128)(2,1)}, /*...) while((s32[]{:T(128)}, f32[1,8,256]{2,1,0:T(8,128)S(1)}, ...), condition=%wide.region_4.5_spmd.clone, body=%wide.region_1.4_spmd.clone.sunk | while | flops 139470848 | bytes 10330286 | solution.py:101
  115.0 2.7 bitcast_reduce_fusion.2
  117.7 3.0 %fusion.86 = f32[8,256]{1,0:T(8,128)S(1)} fusion(f32[8,512,256]{2,1,0:T(8,128)} %get-tuple-element.514, f32[8,256]{1,0:T(8,128)S(1)} %bitcast.239), kind=kLoop, calls=%fused_computation.3.clone.1 | loop fusion | flops 3143680 | bytes 4210688 | tf_op jit(solution)/shard_map/while/body/eval_jaxpr/reduce_sum | solution.py:95
  123.1 2.7 bitcast_reduce_fusion.2
  125.8 2.9 %fusion.86 = f32[8,256]{1,0:T(8,128)S(1)} fusion(f32[8,512,256]{2,1,0:T(8,128)} %get-tuple-element.514, f32[8,256]{1,0:T(8,128)S(1)} %bitcast.239), kind=kLoop, calls=%fused_computation.3.clone.1 | loop fusion | flops 3143680 | bytes 4210688 | tf_op jit(solution)/shard_map/while/body/eval_jaxpr/reduce_sum | solution.py:95
  128.7 10.6 %all-gather.7.cloned.1.call-done = bf16[1,1024,1,512]{3,1,2,0:T(8,128)(2,1)} async-done(((bf16[1,256,1,512]{3,1,2,0:T(8,128)(2,1)}), bf16[1,1024,1,512]{3,1,2,0:T(8,128)(2,1)}) %all-gather.7.cloned.1.call-update) | async-done | bytes 1048592 | tf_op jit(solution)/shard_map/all_gather | solution.py:72
  139.4 2.3 copy.54
  141.7 13.9 %while.38 = (s32[]{:T(128)}, f32[1,256,8,64]{1,3,2,0:T(8,128)}, s32[2]{0:T(128)S(1)}, bf16[1,1024,512]{1,2,0:T(8,128)(2,1)}, bf16[1,1024,512]{1,2,0:T(8,128)(2,1...) while((s32[]{:T(128)}, f32[1,256,8,64]{1,3,2,0:T(8,128)}, ...), condition=%wide.region_6.7_spmd.clone, body=%wide.region_5.6_spmd.clone.sunk | while | flops 272891904 | bytes 4473021 | solution.py:116
  142.9 2.3 constant_dynamic-slice_fusion.9
  145.2 3.4 %fusion.90 = f32[1,256,8,64]{1,3,2,0:T(8,128)} fusion(bf16[512,8,64]{0,2,1:T(8,128)(2,1)} %bitcast.236, bf16[512,8,64]{0,2,1:T(8,128)(2,1)} %bitcast.235, f32[8,256]{1,0:T(8,128)S(1)} %bitcast.249, f32[8,256]{1,0:T(8,128)S(1)} %bitcast.245, f32[1,256,8,64]{1,3,2,0:T(8,128)} %get-tuple-element.581, ...), kind=kOutput, calls=%fused_computation.13.clone.1 | convolution fusion | flops 272891904 | bytes 2375681 | tf_op jit(solution)/shard_map/while/body/eval_jaxpr/chfk,ckhe->cfhe/dot_general | solution.py:111
  149.8 2.3 constant_dynamic-slice_fusion.9
  152.0 3.6 %fusion.90 = f32[1,256,8,64]{1,3,2,0:T(8,128)} fusion(bf16[512,8,64]{0,2,1:T(8,128)(2,1)} %bitcast.236, bf16[512,8,64]{0,2,1:T(8,128)(2,1)} %bitcast.235, f32[8,256]{1,0:T(8,128)S(1)} %bitcast.249, f32[8,256]{1,0:T(8,128)S(1)} %bitcast.245, f32[1,256,8,64]{1,3,2,0:T(8,128)} %get-tuple-element.581, ...), kind=kOutput, calls=%fused_computation.13.clone.1 | convolution fusion | flops 272891904 | bytes 2375681 | tf_op jit(solution)/shard_map/while/body/eval_jaxpr/chfk,ckhe->cfhe/dot_general | solution.py:111
  160.3 31.9 %psum.7 = f32[2]{0:T(128)S(1)} all-reduce(f32[2]{0:T(128)S(1)} %compare_select_fusion.2), channel_id=1, replica_groups=mesh['groups'=2,'seq'=4,'mp'=2,'section'=2] {'seq','mp','section'}, use_global_device_ids=true, to_apply=%region_8.9 | all-reduce | flops 2 | bytes 16 | tf_op jit(solution)/shard_map/psum | solution.py:128
  198.3 25.0 %while.39 = (s32[]{:T(128)}, f32[1,256,8,64]{1,3,2,0:T(8,128)}, bf16[2,512,1,1024]{1,3,2,0:T(8,128)(2,1)}, s32[2]{0:T(128)S(1)}, bf16[1,1024,512]{1,2,0:T(8,128)...) while((s32[]{:T(128)}, f32[1,256,8,64]{1,3,2,0:T(8,128)}, ...), condition=%wide.region_14.15_spmd.clone, body=%wide.region_13.14_spmd.clone.sunk | while | flops 681705472 | bytes 39346984 | solution.py:170
  207.7 3.0 %fusion.101 = f32[1,256,8,64]{1,3,2,0:T(8,128)} fusion(bf16[512,8,64]{0,2,1:T(8,128)(2,1)} %bitcast.227, bf16[8,512,256]{2,1,0:T(8,128)(2,1)} %copy-done.1, f32[1,256,8,64]{1,3,2,0:T(8,128)} %get-tuple-element.620, pred[]{:T(512)S(6)} %compare.19), kind=kOutput, calls=%fused_computation.27.clone.1 | convolution fusion | flops 134610944 | bytes 3670017 | tf_op jit(solution)/shard_map/while/body/eval_jaxpr/chfk,ckhe->cfhe/dot_general | solution.py:151
  220.2 3.1 %fusion.101 = f32[1,256,8,64]{1,3,2,0:T(8,128)} fusion(bf16[512,8,64]{0,2,1:T(8,128)(2,1)} %bitcast.227, bf16[8,512,256]{2,1,0:T(8,128)(2,1)} %copy-done.1, f32[1,256,8,64]{1,3,2,0:T(8,128)} %get-tuple-element.620, pred[]{:T(512)S(6)} %compare.19), kind=kOutput, calls=%fused_computation.27.clone.1 | convolution fusion | flops 134610944 | bytes 3670017 | tf_op jit(solution)/shard_map/while/body/eval_jaxpr/chfk,ckhe->cfhe/dot_general | solution.py:151
  223.3 3.3 %copy.58 = bf16[2,1,128,8,512]{4,3,0,2,1:T(8,128)(2,1)} copy(bf16[2,1,128,8,512]{4,3,2,1,0:T(8,128)(2,1)} %bitcast.70) | data formatting | bytes 4194304 | tf_op jit(solution)/shard_map/reshape | solution.py:171
  227.7 40.2 %reduce-scatter.2.cloned.1.call-done = bf16[256,1,1024]{0,2,1:T(8,128)(2,1)} async-done(((bf16[1024,1,1024]{0,2,1:T(8,128)(2,1)}), bf16[256,1,1024]{0,2,1:T(8,128)(2,1)}) %reduce-scatter.2.cloned.1.call-update) | async-done | bytes 524304 | tf_op jit(solution)/shard_map/reduce_scatter | solution.py:172
  269.9 2.3 copy.56
  (100 shorter events, 49.0 us)
Async XLA Ops:
  7.2 71.4 %copy-start = (bf16[1024,3,512]{2,0,1:T(8,128)(2,1)S(1)}, bf16[1024,3,512]{2,0,1:T(8,128)(2,1)}, u32[]{:S(2)}) copy-start(bf16[1024,3,512]{2,0,1:T(8,128)(2,1)} %param.17) | copy-start | bytes 9437188
  7.2 103.2 %all-gather.5.cloned.1.call-start = ((), (), s32[]{:S(2)}) async-start(), calls=%async_computation.2 | async-start | bytes 1310720 | tf_op jit(solution)/shard_map/all_gather | solution.py:71
  15.8 1.0 copy-start.5
  17.0 9.6 %collective-permute-start = (bf16[1,256,4]{2,1,0:T(8,128)(2,1)S(1)}, bf16[1,256,4]{2,1,0:T(8,128)(2,1)S(1)}, u32[]{:S(2)}, u32[]{:S(2)}) collective-permute-start(bf16[1,256,4]{2,1,0:T(8,128)(2,1)S(1)} %get-tuple-element.365), channel_id=1, source_target_pairs={{0,4},{4,8},{8,12},{1,5},{5,9},{9,13},{2,6},{6,10},{10,14},{3,7},{... | collective-permute-start | bytes 6152 | tf_op jit(solution)/shard_map/ppermute | solution.py:18
  21.9 6.2 %collective-permute-start.1 = (bf16[1,256,4]{2,1,0:T(8,128)(2,1)S(1)}, bf16[1,256,4]{2,1,0:T(8,128)(2,1)S(1)}, u32[]{:S(2)}, u32[]{:S(2)}) collective-permute-start(bf16[1,256,4]{2,1,0:T(8,128)(2,1)S(1)} %get-tuple-element.364), channel_id=1, source_target_pairs={{4,0},{8,4},{12,8},{5,1},{9,5},{13,9},{6,2},{10,6},{14,10},{7,3},{... | collective-permute-start | bytes 6152 | tf_op jit(solution)/shard_map/ppermute | solution.py:21
  61.7 1.9 copy-start.6
  70.4 0.7 copy-start.7
  78.6 2.1 copy-start.9
  80.6 58.8 %all-gather.7.cloned.1.call-start = ((), (), s32[]{:S(2)}) async-start(), calls=%async_computation.3 | async-start | bytes 1310720 | tf_op jit(solution)/shard_map/all_gather | solution.py:72
  81.8 186.0 %reduce-scatter.2.cloned.1.call-start = ((), (), s32[]{:S(2)}) async-start(), calls=%async_computation.1 | async-start | bytes 2621440 | tf_op jit(solution)/shard_map/reduce_scatter | solution.py:172
  141.7 16.1 %copy-start.8 = (f32[512]{0:T(512)S(1)}, f32[512]{0:T(512)}, u32[]{:S(2)}) copy-start(f32[512]{0:T(512)} %param.18) | copy-start | bytes 6148
  141.7 50.6 %copy-start.10 = (s32[4]{0:T(128)S(1)}, s32[4]{0:T(128)}, u32[]{:S(2)}) copy-start(s32[4]{0:T(128)} %param.21) | copy-start | bytes 52
  155.6 38.7 %copy-start.3 = (bf16[1,256,8,64]{1,3,2,0:T(8,128)(2,1)}, bf16[1,256,8,64]{1,3,2,0:T(8,128)(2,1)S(1)}, u32[]{:S(2)}) copy-start(bf16[1,256,8,64]{1,3,2,0:T(8,128)(2,1)S(1)} %get-tuple-element.656) | copy-start | bytes 786436
  192.2 6.1 %copy-start.11 = (f32[2]{0:T(128)}, f32[2]{0:T(128)S(1)}, u32[]{:S(2)}) copy-start(f32[2]{0:T(128)S(1)} %psum.7) | copy-start | bytes 28
  200.8 2.2 copy-start.2
  203.0 2.1 copy-start.4
  203.8 1.3 copy-start.1
  213.3 2.2 copy-start.2
  215.5 2.1 copy-start.4
  216.3 1.3 copy-start.1
Sparse Core Ops, SparseCore 0:
  80.7 29.6 all-gather.4
  111.9 27.4 all-gather.6
  226.7 41.0 reduce-scatter.1
where the time goes:
time: 280 us; the launch traced here: 279 us
  waiting for transfers between devices  80.7 us (29%)
  local copies, waits for them, and re-layouts  71.9 us (26%)
  blocking collectives  39.2 us (14%)
  other arithmetic  31.1 us (11%)
  matrix products  29.7 us (11%)
  between operations  15.3 us (5%)
  starting transfers between devices  6.74 us (2%)
  loops' own time  4.08 us (1%)
    reduce_scatter x1, waiting for transfers between devices, local(): lax.psum_scatter(stacked.astype(f32).astype(jnp.bfloat16), 'seq', scatter...  40.2 us
    psum x1, blocking collectives, local(): lax.psum(jnp.sum(owner * partial_rewards[:, None], axis=0), ('seq', 'mp',...  31.9 us
    all_gather x1, waiting for transfers between devices, local(): lax.all_gather(qkv[:, :, 1], 'seq', axis=1, tiled=True)  28.3 us
    slice x2, local copies, waits for them, and re-layouts, local(): blocks[:, :, :-1]  14.2 us
    all_gather x1, waiting for transfers between devices, local(): lax.all_gather(qkv[:, :, 2], 'seq', axis=1, tiled=True)  10.6 us
    dot_general x4, matrix products, scores_for(): jnp.einsum('cfhe,ckhe->chfk', query4, key_slice(keys, start, size), prefe...  9.74 us
    dynamic_slice x6, local copies, waits for them, and re-layouts, key_slice(): lax.dynamic_slice_in_dim(source, start, size, 1)  9.22 us
    unnamed x21, local copies, waits for them, and re-layouts  8.64 us
  transfers between devices with their start and end apart: 5, of which 4 were waited for; matrix products, arithmetic and copies ran while one was open for 8% of the time, Pallas kernels for 0%

commit v1 on v0

--- a/solution.py
+++ b/solution.py
@@ -125,7 +125,10 @@
         == (section_id * cand + jnp.arange(cand, dtype=jnp.int32))[:, None]
     ).astype(f32)
     partial_rewards = jnp.sum(attended * gate * readout, axis=(1, 2)) / math.sqrt(total)
-    rewards = lax.psum(jnp.sum(owner * partial_rewards[:, None], axis=0), ("seq", "mp", "section"))
+    rewards = jnp.sum(
+        lax.all_gather(jnp.sum(owner * partial_rewards[:, None], axis=0), ("seq", "mp", "section")),
+        axis=0,
+    )
     chosen = (pairs[:, :, None] == jnp.arange(all_cands, dtype=jnp.int32)[None, None, :]).astype(
         f32
     )

time: 280 us -> 268 us (0.957)
  blocking collectives: 39.2 us -> 27.1 us
    psum x1 -> x0, blocking collectives: 31.9 us -> none  [local(): lax.psum(jnp.sum(owner * partial_rewards[:, None], axis=0), ('seq', 'mp',...]
    all_gather x0 -> x1, blocking collectives: none -> 19.8 us  [local(): lax.all_gather(jnp.sum(owner * partial_rewards[:, None], axis=0), ('seq',...]
where the time goes in v1:
time: 268 us; the launch traced here: 267 us
  waiting for transfers between devices  80.7 us (30%)
  local copies, waits for them, and re-layouts  71.9 us (27%)
  other arithmetic  31.2 us (12%)
  matrix products  29.7 us (11%)
  blocking collectives  27.1 us (10%)
  between operations  15.3 us (6%)
  starting transfers between devices  6.74 us (3%)
  loops' own time  4.08 us (2%)
    reduce_scatter x1, waiting for transfers between devices, local(): lax.psum_scatter(stacked.astype(f32).astype(jnp.bfloat16), 'seq', scatter...  40.2 us
    all_gather x1, waiting for transfers between devices, local(): lax.all_gather(qkv[:, :, 1], 'seq', axis=1, tiled=True)  28.3 us
    all_gather x1, blocking collectives, local(): lax.all_gather(jnp.sum(owner * partial_rewards[:, None], axis=0), ('seq',...  19.8 us
    slice x2, local copies, waits for them, and re-layouts, local(): blocks[:, :, :-1]  14.2 us
    all_gather x1, waiting for transfers between devices, local(): lax.all_gather(qkv[:, :, 2], 'seq', axis=1, tiled=True)  10.6 us
    dot_general x4, matrix products, scores_for(): jnp.einsum('cfhe,ckhe->chfk', query4, key_slice(keys, start, size), prefe...  9.74 us
    dynamic_slice x6, local copies, waits for them, and re-layouts, key_slice(): lax.dynamic_slice_in_dim(source, start, size, 1)  9.22 us
    unnamed x21, local copies, waits for them, and re-layouts  8.64 us
  transfers between devices with their start and end apart: 5, of which 4 were waited for; matrix products, arithmetic and copies ran while one was open for 8% of the time, Pallas kernels for 0%

profile of v1, /device:TPU:0, one launch (start us, length us, event | category | flops | bytes accessed | tf_op | source)
XLA Modules:
  0.0 266.6 jit_solution(14954498086270851896)
XLA Ops:
  7.2 8.6 %fusion.25 = bf16[1,256,2048]{2,1,0:T(8,128)(2,1)S(1)} fusion(bf16[1,256,2048]{2,1,0:T(8,128)(2,1)} %param.14, f32[256]{0:T(256)} %param.15), kind=kLoop, calls=%fused_computation.40 | loop fusion | flops 3145728 | bytes 2098176 | tf_op jit(solution)/shard_map/convert_element_type | solution.py:46
  17.0 4.9 %collective-permute-start = (bf16[1,256,4]{2,1,0:T(8,128)(2,1)S(1)}, bf16[1,256,4]{2,1,0:T(8,128)(2,1)S(1)}, u32[]{:S(2)}, u32[]{:S(2)}) collective-permute-start(bf16[1,256,4]{2,1,0:T(8,128)(2,1)S(1)} %get-tuple-element.365), channel_id=1, source_target_pairs={{0,4},{4,8},{8,12},{1,5},{5,9},{9,13},{2,6},{6,10},{10,14},{3,7},{... | collective-permute-start | bytes 6152 | tf_op jit(solution)/shard_map/ppermute | solution.py:18
  24.1 2.4 reshape.448
  28.1 3.5 %concatenate.32 = bf16[1,256,2056]{2,1,0:T(8,128)(2,1)} concatenate(bf16[1,256,4]{2,1,0:T(8,128)(2,1)S(1)} %collective-permute-done, bf16[1,256,2048]{2,1,0:T(8,128)(2,1)} %copy-done.5, bf16[1,256,4]{2,1,0:T(8,128)(2,1)S(1)} %collective-permute-done.1), dimensions={2} | concatenate | bytes 2105344 | tf_op jit(solution)/shard_map/concatenate | solution.py:22
  31.6 2.3 copy.41
  33.9 5.8 %reshape.446 = bf16[1,8,32,257,8]{2,1,4,3,0:T(8,128)(2,1)} reshape(bf16[1,256,2056]{1,2,0:T(8,128)(2,1)} %copy.41) | data formatting | bytes 2105344 | tf_op jit(solution)/shard_map/reshape | solution.py:48
  39.7 6.5 %fusion.54 = (bf16[1,8,256,32,8]{3,1,4,2,0:T(8,128)(2,1)}, bf16[1,8,256,32,8]{3,1,4,2,0:T(8,128)(2,1)}) fusion(bf16[1,8,257,32,8]{3,1,4,2,0:T(8,128)(2,1)} %bitcast.235), kind=kLoop, calls=%fused_computation.103 | loop fusion | bytes 4194304 | tf_op jit(solution)/shard_map/slice | solution.py:51
  46.2 7.7 %copy.42 = bf16[1,8,256,32,8]{2,4,3,1,0:T(8,128)(2,1)} copy(bf16[1,8,256,32,8]{3,1,4,2,0:T(8,128)(2,1)} %get-tuple-element.362) | data formatting | bytes 2097152 | tf_op jit(solution)/shard_map/slice | solution.py:51
  53.9 7.7 %copy.43 = bf16[1,8,256,32,8]{2,4,3,1,0:T(8,128)(2,1)} copy(bf16[1,8,256,32,8]{3,1,4,2,0:T(8,128)(2,1)} %get-tuple-element.363) | data formatting | bytes 2097152 | tf_op jit(solution)/shard_map/slice | solution.py:51
  66.9 3.5 %fusion.31 = bf16[1,256,512]{2,1,0:T(8,128)(2,1)S(1)} fusion(f32[1,256,512]{2,1,0:T(8,128)} %copy.46, f32[512]{0:T(512)S(1)} %fusion.36, f32[256]{0:T(256)S(1)} %add_convert_fusion, pred[512]{0:T(512)(128)(4,1)S(1)} %fusion.33), kind=kLoop, calls=%fused_computation.52 | loop fusion | flops 524288 | bytes 790016 | tf_op jit(solution)/shard_map/convert_element_type | solution.py:64
  71.1 7.3 %all_gather.13 = bf16[1,256,1024]{2,1,0:T(8,128)(2,1)S(1)} all-gather(bf16[1,256,512]{2,1,0:T(8,128)(2,1)S(1)} %fusion.31), channel_id=1, replica_groups=mesh['groups'=2,'seq'=4,'mp'=2,'section'=2] {'mp'}, dimensions={2}, use_global_device_ids=true | all-gather | bytes 786432 | tf_op jit(solution)/shard_map/all_gather | solution.py:65
  82.1 28.3 %all-gather.6.cloned.1.call-done = bf16[1,1024,1,512]{3,1,2,0:T(8,128)(2,1)} async-done(((bf16[1,256,1,512]{3,1,2,0:T(8,128)(2,1)}), bf16[1,1024,1,512]{3,1,2,0:T(8,128)(2,1)}) %all-gather.6.cloned.1.call-update) | async-done | bytes 1048592 | tf_op jit(solution)/shard_map/all_gather | solution.py:71
  110.4 2.3 copy.53
  112.6 16.1 %while.37 = (s32[]{:T(128)}, f32[1,8,256]{2,1,0:T(8,128)S(1)}, f32[1,8,256]{2,1,0:T(8,128)S(1)}, s32[2]{0:T(128)S(1)}, bf16[1,1024,512]{1,2,0:T(8,128)(2,1)}, /*...) while((s32[]{:T(128)}, f32[1,8,256]{2,1,0:T(8,128)S(1)}, ...), condition=%wide.region_4.5_spmd.clone, body=%wide.region_1.4_spmd.clone.sunk | while | flops 139470848 | bytes 10330286 | solution.py:101
  115.0 2.7 %bitcast_reduce_fusion.2 = (f32[8,256]{1,0:T(8,128)S(1)}, f32[8,512,256]{2,1,0:T(8,128)}) fusion(bf16[512,8,64]{0,2,1:T(8,128)(2,1)S(1)} %bitcast.230, bf16[1,256,8,64]{1,3,2,0:T(8,128)(2,1)S(1)} %get-tuple-element.563), kind=kOutput, calls=%fused_computation.1.clone.1 | convolution fusion | flops 136312832 | bytes 4988928 | tf_op jit(solution)/shard_map/while/body/eval_jaxpr/cfhe,ckhe->chfk/dot_general | solution.py:85
  117.7 3.0 %fusion.87 = f32[8,256]{1,0:T(8,128)S(1)} fusion(f32[8,512,256]{2,1,0:T(8,128)} %get-tuple-element.514, f32[8,256]{1,0:T(8,128)S(1)} %bitcast.241), kind=kLoop, calls=%fused_computation.3.clone.1 | loop fusion | flops 3143680 | bytes 4210688 | tf_op jit(solution)/shard_map/while/body/eval_jaxpr/reduce_sum | solution.py:95
  123.1 2.7 %bitcast_reduce_fusion.2 = (f32[8,256]{1,0:T(8,128)S(1)}, f32[8,512,256]{2,1,0:T(8,128)}) fusion(bf16[512,8,64]{0,2,1:T(8,128)(2,1)S(1)} %bitcast.230, bf16[1,256,8,64]{1,3,2,0:T(8,128)(2,1)S(1)} %get-tuple-element.563), kind=kOutput, calls=%fused_computation.1.clone.1 | convolution fusion | flops 136312832 | bytes 4988928 | tf_op jit(solution)/shard_map/while/body/eval_jaxpr/cfhe,ckhe->chfk/dot_general | solution.py:85
  125.8 2.9 %fusion.87 = f32[8,256]{1,0:T(8,128)S(1)} fusion(f32[8,512,256]{2,1,0:T(8,128)} %get-tuple-element.514, f32[8,256]{1,0:T(8,128)S(1)} %bitcast.241), kind=kLoop, calls=%fused_computation.3.clone.1 | loop fusion | flops 3143680 | bytes 4210688 | tf_op jit(solution)/shard_map/while/body/eval_jaxpr/reduce_sum | solution.py:95
  128.7 10.6 %all-gather.8.cloned.1.call-done = bf16[1,1024,1,512]{3,1,2,0:T(8,128)(2,1)} async-done(((bf16[1,256,1,512]{3,1,2,0:T(8,128)(2,1)}), bf16[1,1024,1,512]{3,1,2,0:T(8,128)(2,1)}) %all-gather.8.cloned.1.call-update) | async-done | bytes 1048592 | tf_op jit(solution)/shard_map/all_gather | solution.py:72
  139.4 2.3 copy.54
  141.7 13.9 %while.38 = (s32[]{:T(128)}, f32[1,256,8,64]{1,3,2,0:T(8,128)}, s32[2]{0:T(128)S(1)}, bf16[1,1024,512]{1,2,0:T(8,128)(2,1)}, bf16[1,1024,512]{1,2,0:T(8,128)(2,1...) while((s32[]{:T(128)}, f32[1,256,8,64]{1,3,2,0:T(8,128)}, ...), condition=%wide.region_6.7_spmd.clone, body=%wide.region_5.6_spmd.clone.sunk | while | flops 272891904 | bytes 4473021 | solution.py:116
  142.9 2.3 constant_dynamic-slice_fusion.9
  145.2 3.4 %fusion.91 = f32[1,256,8,64]{1,3,2,0:T(8,128)} fusion(bf16[512,8,64]{0,2,1:T(8,128)(2,1)} %bitcast.238, bf16[512,8,64]{0,2,1:T(8,128)(2,1)} %bitcast.237, f32[8,256]{1,0:T(8,128)S(1)} %bitcast.251, f32[8,256]{1,0:T(8,128)S(1)} %bitcast.247, f32[1,256,8,64]{1,3,2,0:T(8,128)} %get-tuple-element.581, ...), kind=kOutput, calls=%fused_computation.13.clone.1 | convolution fusion | flops 272891904 | bytes 2375681 | tf_op jit(solution)/shard_map/while/body/eval_jaxpr/chfk,ckhe->cfhe/dot_general | solution.py:111
  149.8 2.3 constant_dynamic-slice_fusion.9
  152.0 3.6 %fusion.91 = f32[1,256,8,64]{1,3,2,0:T(8,128)} fusion(bf16[512,8,64]{0,2,1:T(8,128)(2,1)} %bitcast.238, bf16[512,8,64]{0,2,1:T(8,128)(2,1)} %bitcast.237, f32[8,256]{1,0:T(8,128)S(1)} %bitcast.251, f32[8,256]{1,0:T(8,128)S(1)} %bitcast.247, f32[1,256,8,64]{1,3,2,0:T(8,128)} %get-tuple-element.581, ...), kind=kOutput, calls=%fused_computation.13.clone.1 | convolution fusion | flops 272891904 | bytes 2375681 | tf_op jit(solution)/shard_map/while/body/eval_jaxpr/chfk,ckhe->cfhe/dot_general | solution.py:111
  160.3 19.8 %all-gather.2 = f32[16,1,2]{2,1,0:T(1,128)S(1)} all-gather(f32[1,1,2]{2,1,0:T(1,128)S(1)} %fusion.45), channel_id=1, replica_groups=mesh['groups'=2,'seq'=4,'mp'=2,'section'=2] {'seq','mp','section'}, dimensions={0}, use_global_device_ids=true | all-gather | bytes 136 | tf_op jit(solution)/shard_map/all_gather | solution.py:129
  186.2 25.0 %while.39 = (s32[]{:T(128)}, f32[1,256,8,64]{1,3,2,0:T(8,128)}, bf16[2,512,1,1024]{1,3,2,0:T(8,128)(2,1)}, s32[2]{0:T(128)S(1)}, bf16[1,1024,512]{1,2,0:T(8,128)...) while((s32[]{:T(128)}, f32[1,256,8,64]{1,3,2,0:T(8,128)}, ...), condition=%wide.region_14.15_spmd.clone, body=%wide.region_13.14_spmd.clone.sunk | while | flops 681705472 | bytes 39346984 | solution.py:173
  195.6 3.0 %fusion.102 = f32[1,256,8,64]{1,3,2,0:T(8,128)} fusion(bf16[512,8,64]{0,2,1:T(8,128)(2,1)} %bitcast.229, bf16[8,512,256]{2,1,0:T(8,128)(2,1)} %copy-done.1, f32[1,256,8,64]{1,3,2,0:T(8,128)} %get-tuple-element.620, pred[]{:T(512)S(6)} %compare.19), kind=kOutput, calls=%fused_computation.27.clone.1 | convolution fusion | flops 134610944 | bytes 3670017 | tf_op jit(solution)/shard_map/while/body/eval_jaxpr/chfk,ckhe->cfhe/dot_general | solution.py:154
  208.1 3.1 %fusion.102 = f32[1,256,8,64]{1,3,2,0:T(8,128)} fusion(bf16[512,8,64]{0,2,1:T(8,128)(2,1)} %bitcast.229, bf16[8,512,256]{2,1,0:T(8,128)(2,1)} %copy-done.1, f32[1,256,8,64]{1,3,2,0:T(8,128)} %get-tuple-element.620, pred[]{:T(512)S(6)} %compare.19), kind=kOutput, calls=%fused_computation.27.clone.1 | convolution fusion | flops 134610944 | bytes 3670017 | tf_op jit(solution)/shard_map/while/body/eval_jaxpr/chfk,ckhe->cfhe/dot_general | solution.py:154
  211.2 3.3 %copy.58 = bf16[2,1,128,8,512]{4,3,0,2,1:T(8,128)(2,1)} copy(bf16[2,1,128,8,512]{4,3,2,1,0:T(8,128)(2,1)} %bitcast.71) | data formatting | bytes 4194304 | tf_op jit(solution)/shard_map/reshape | solution.py:174
  215.6 40.2 %reduce-scatter.2.cloned.1.call-done = bf16[256,1,1024]{0,2,1:T(8,128)(2,1)} async-done(((bf16[1024,1,1024]{0,2,1:T(8,128)(2,1)}), bf16[256,1,1024]{0,2,1:T(8,128)(2,1)}) %reduce-scatter.2.cloned.1.call-update) | async-done | bytes 524304 | tf_op jit(solution)/shard_map/reduce_scatter | solution.py:175
  257.8 2.3 copy.56
  (101 shorter events, 49.0 us)
Async XLA Ops:
  7.2 71.4 %copy-start = (bf16[1024,3,512]{2,0,1:T(8,128)(2,1)S(1)}, bf16[1024,3,512]{2,0,1:T(8,128)(2,1)}, u32[]{:S(2)}) copy-start(bf16[1024,3,512]{2,0,1:T(8,128)(2,1)} %param.17) | copy-start | bytes 9437188
  7.2 103.2 %all-gather.6.cloned.1.call-start = ((), (), s32[]{:S(2)}) async-start(), calls=%async_computation.2 | async-start | bytes 1310720 | tf_op jit(solution)/shard_map/all_gather | solution.py:71
  15.8 1.0 copy-start.5
  17.0 9.6 %collective-permute-start = (bf16[1,256,4]{2,1,0:T(8,128)(2,1)S(1)}, bf16[1,256,4]{2,1,0:T(8,128)(2,1)S(1)}, u32[]{:S(2)}, u32[]{:S(2)}) collective-permute-start(bf16[1,256,4]{2,1,0:T(8,128)(2,1)S(1)} %get-tuple-element.365), channel_id=1, source_target_pairs={{0,4},{4,8},{8,12},{1,5},{5,9},{9,13},{2,6},{6,10},{10,14},{3,7},{... | collective-permute-start | bytes 6152 | tf_op jit(solution)/shard_map/ppermute | solution.py:18
  21.9 6.2 %collective-permute-start.1 = (bf16[1,256,4]{2,1,0:T(8,128)(2,1)S(1)}, bf16[1,256,4]{2,1,0:T(8,128)(2,1)S(1)}, u32[]{:S(2)}, u32[]{:S(2)}) collective-permute-start(bf16[1,256,4]{2,1,0:T(8,128)(2,1)S(1)} %get-tuple-element.364), channel_id=1, source_target_pairs={{4,0},{8,4},{12,8},{5,1},{9,5},{13,9},{6,2},{10,6},{14,10},{7,3},{... | collective-permute-start | bytes 6152 | tf_op jit(solution)/shard_map/ppermute | solution.py:21
  61.7 1.9 copy-start.6
  70.4 0.7 copy-start.7
  78.6 2.1 copy-start.9
  80.6 58.8 %all-gather.8.cloned.1.call-start = ((), (), s32[]{:S(2)}) async-start(), calls=%async_computation.3 | async-start | bytes 1310720 | tf_op jit(solution)/shard_map/all_gather | solution.py:72
  81.8 174.0 %reduce-scatter.2.cloned.1.call-start = ((), (), s32[]{:S(2)}) async-start(), calls=%async_computation.1 | async-start | bytes 2621440 | tf_op jit(solution)/shard_map/reduce_scatter | solution.py:175
  141.7 16.1 %copy-start.8 = (f32[512]{0:T(512)S(1)}, f32[512]{0:T(512)}, u32[]{:S(2)}) copy-start(f32[512]{0:T(512)} %param.18) | copy-start | bytes 6148
  141.7 38.5 %copy-start.11 = (s32[4]{0:T(128)S(1)}, s32[4]{0:T(128)}, u32[]{:S(2)}) copy-start(s32[4]{0:T(128)} %param.21) | copy-start | bytes 52
  155.6 26.6 %copy-start.3 = (bf16[1,256,8,64]{1,3,2,0:T(8,128)(2,1)}, bf16[1,256,8,64]{1,3,2,0:T(8,128)(2,1)S(1)}, u32[]{:S(2)}) copy-start(bf16[1,256,8,64]{1,3,2,0:T(8,128)(2,1)S(1)} %get-tuple-element.656) | copy-start | bytes 786436
  180.1 6.1 %copy-start.10 = (f32[2]{0:T(128)}, f32[2]{0:T(128)S(1)}, u32[]{:S(2)}) copy-start(f32[2]{0:T(128)S(1)} %reduce_sum.91) | copy-start | bytes 28
  188.8 2.2 copy-start.2
  191.0 2.1 copy-start.4
  191.7 1.3 copy-start.1
  201.2 2.2 copy-start.2
  203.4 2.1 copy-start.4
  204.2 1.3 copy-start.1
Sparse Core Ops, SparseCore 0:
  80.7 29.6 all-gather.5
  111.9 27.4 all-gather.7
  214.6 41.0 reduce-scatter.1
